TPU v7x, 32 devices: a whole 2x2x4 slice. The times are simulated.
32 devices in a mesh: harm: 16 (over z, x, core), bus: 2 (over y).
Axes of the slice: x: 2, y: 2, z: 4, core: 2. Of those that a mesh axis runs over, the one named last changes fastest.
Arguments:
- conv_volt: bfloat16 [2, 64, 128, 128], P(None, None, ('bus', 'harm')), may hold values from -0.75 to 0.75
- conv_power: float32 [128, 128], P(('bus', 'harm')), may hold values from 0.2 to 2
- conv_type: int32 [128], P(('bus', 'harm')), may hold values from 0 to 7
- type_steep: float32 [8], replicated, may hold values from 0.5 to 4
- conv_bus: int32 [128], P(('bus', 'harm')), may hold values from 0 to 511, as said below
- admittance: float32 [2, 4, 64, 512], P(None, None, 'harm', 'bus'), may hold values from -0.5 to 1
- link_offset: int32 [3, 512], P(None, 'bus'), may hold values from -8 to 8, as said below
Outputs:
- bus_volt: bfloat16 [2, 64, 512, 128], P(None, 'harm', 'bus')
- conv_next: bfloat16 [2, 64, 128, 128], P(None, None, ('bus', 'harm'))
Inputs may be any that keep to these rules, and one draw needn't show every extreme that they name: `conv_bus`: converter c is attached to one of the buses from (c // 4) * 16 to (c // 4 + 1) * 16 - 1; a bus may carry several converters. `link_offset`: the first line of every bus spans exactly 8 buses, up or down; the others span 1 to 8 buses; no offset is zero.
All inputs are finite; a program needn't handle non-finite values.
Results may differ from a plain program's by a relative error of at most 0.0057.
Values may be sent and summed in bfloat16 or wider, within the bound.
A program may use at most 64 MiB of HBM per device.

v0:
```python
import math
import jax
import jax.numpy as jnp
from jax import lax
from jax.sharding import PartitionSpec as P

H = 64
NT = 1024
REACH = 8
ITERS = 3


def as_sent(array):
    return jax.tree.map(lambda a: a.astype(jnp.bfloat16) if a.dtype == jnp.float32 else a, array)


def extended_2(cells, sides, width):
    for axis, dim in sides:
        count = lax.axis_size(axis)
        ends = count - 1
        head = lax.slice_in_dim(cells, 0, width, axis=dim)
        tail = lax.slice_in_dim(cells, cells.shape[dim] - width, cells.shape[dim], axis=dim)
        cells = jnp.concatenate(
            [
                lax.ppermute(tail, axis, [(i, (i + 1) % count) for i in range(ends)]),
                cells,
                lax.ppermute(head, axis, [((i + 1) % count, i) for i in range(ends)]),
            ],
            axis=dim,
        )
    return cells


def make_basis():
    orders = jnp.arange(1, H + 1, dtype=jnp.int32)
    samples = jnp.arange(NT, dtype=jnp.int32)
    phases = (orders[:, None] * samples[None, :] % NT).astype(jnp.float32) * (2.0 * math.pi / NT)
    return jnp.concatenate([jnp.cos(phases), -jnp.sin(phases)], axis=0).astype(jnp.bfloat16)


def complex_product(left_real, left_imag, right_real, right_imag):
    return (
        left_real * right_real - left_imag * right_imag,
        left_real * right_imag + left_imag * right_real,
    )


def line_sum(inject_real, inject_imag, volt_real, volt_imag, lines_real, lines_imag, targets):
    total_real, total_imag = (inject_real, inject_imag)
    for line_num in range(targets.shape[0]):
        near_real = jnp.take(volt_real, targets[line_num], axis=1)
        near_imag = jnp.take(volt_imag, targets[line_num], axis=1)
        term_real, term_imag = complex_product(
            lines_real[line_num][:, :, None], lines_imag[line_num][:, :, None], near_real, near_imag
        )
        total_real = total_real + term_real
        total_imag = total_imag + term_imag
    return (total_real, total_imag)


def local(conv_volt, conv_power, conv_type, type_steep, conv_bus, admittance, link_offset):
    block_rows = admittance.shape[3]
    conv_count = conv_volt.shape[2]
    snapshots = conv_volt.shape[3]
    first_bus = lax.axis_index("bus") * block_rows
    harmonic_basis = make_basis()
    matches = conv_type[:, None] == jnp.arange(type_steep.shape[0], dtype=jnp.int32)[None, :]
    steepness = jnp.sum(jnp.where(matches, type_steep[None, :], 0.0), axis=1)
    volt_rows = conv_volt.reshape(2 * H, conv_count, snapshots)
    block_size = min(conv_count, 4)
    waveform = jnp.einsum(
        "kcs,kn->csn", volt_rows, harmonic_basis, preferred_element_type=jnp.float32
    )
    current = (
        conv_power[0:block_size, :, None] * jnp.tanh(steepness[0:block_size, None, None] * waveform)
    ).astype(jnp.bfloat16)
    spectra = jnp.einsum(
        "csn,kn->kcs", current, harmonic_basis, preferred_element_type=jnp.float32
    ) * NT ** (-0.5)
    pieces = spectra.astype(jnp.bfloat16)
    spectra = pieces.reshape(2, H, conv_count, snapshots)
    received = lax.all_to_all(spectra, "harm", split_axis=1, concat_axis=2, tiled=True)
    block_bus = lax.all_gather(conv_bus, "harm", axis=0, tiled=True) - first_bus
    summed = (
        jnp.zeros((2, received.shape[1], block_rows, snapshots), jnp.float32)
        .at[:, :, block_bus, :]
        .add(received.astype(jnp.float32))
    )
    injection = summed.astype(jnp.bfloat16)
    inject_real = injection[0].astype(jnp.float32)
    inject_imag = injection[1].astype(jnp.float32)
    inverse_real = admittance[0, 0][:, :, None]
    inverse_imag = admittance[1, 0][:, :, None]
    volt_real, volt_imag = complex_product(inverse_real, inverse_imag, inject_real, inject_imag)
    targets = jnp.arange(block_rows, dtype=jnp.int32)[None, :] + REACH + link_offset
    for sweep_index in range(ITERS - 1):
        extended = extended_2(as_sent(jnp.stack([volt_real, volt_imag])), (("bus", 2),), REACH)
        total_real, total_imag = line_sum(
            inject_real,
            inject_imag,
            extended[0],
            extended[1],
            admittance[0, 1:],
            admittance[1, 1:],
            targets,
        )
        volt_real, volt_imag = complex_product(inverse_real, inverse_imag, total_real, total_imag)
    bus_volt = jnp.stack([volt_real, volt_imag]).astype(jnp.bfloat16)
    picked = jnp.take(bus_volt, block_bus, axis=2)
    conv_next = lax.all_to_all(picked, "harm", split_axis=2, concat_axis=1, tiled=True)
    return (bus_volt, conv_next)


def solution(mesh):
    in_specs = (
        P(None, None, ("bus", "harm"), None),
        P(("bus", "harm"), None),
        P(("bus", "harm")),
        P(),
        P(("bus", "harm")),
        P(None, None, "harm", "bus"),
        P(None, "bus"),
    )
    out_specs = (P(None, "harm", "bus", None), P(None, None, ("bus", "harm"), None))
    return jax.shard_map(local, mesh=mesh, in_specs=in_specs, out_specs=out_specs, check_vma=False)
```

profile of v0, /device:TPU:0, one launch (start us, length us, event | category | flops | bytes accessed | tf_op | source)
XLA Modules:
  0.0 89.9 jit_solution(17024910230587955081)
XLA Ops:
  0.7 1.2 %cosine_convert_fusion = (bf16[64,1024]{1,0:T(8,128)(2,1)S(1)}, bf16[64,1024]{1,0:T(8,128)(2,1)S(1)}) fusion(s32[64]{0:T(128)S(1)} %iota_add_fusion.1), kind=kLoop, calls=%fused_computation.105 | loop fusion | flops 1114112 | bytes 262400 | tf_op jit(solution)/shard_map/convert.15
  1.9 0.9 select_reduce_fusion
  2.8 1.3 %fusion.3 = bf16[128,4,128]{2,0,1:T(8,128)(2,1)S(1)} fusion(f32[4]{0:T(128)S(1)} %select_reduce_fusion, f32[4,128]{1,0:T(4,128)} %param.10, bf16[64,1024]{1,0:T(8,128)(2,1)S(1)} %get-tuple-element.41, bf16[64,1024]{1,0:T(8,128)(2,1)S(1)} %get-tuple-element.40, bf16[128,4,128]{2,1,0:T(4,128)(2,1)S(1)} %bitcast.148), kind=kOutput, calls=%fused_computation.18 | convolution fusion | flops 271187968 | bytes 526352 | tf_op jit(solution)/shard_map/csn,kn->kcs/dot_general | solution.py:77
  4.1 0.8 copy.57
  4.9 7.4 %all-to-all-start = ((bf16[2,64,4,128]{3,0,2,1:T(2,128)(2,1)}), bf16[2,64,4,128]{3,0,2,1:T(2,128)(2,1)S(1)}, u32[]{:S(2)}, u32[]{:S(2)}) async-start(bf16[2,64,4,128]{3,0,2,1:T(2,128)(2,1)} %copy.57), calls=%async_computation | async-start | bytes 262144 | tf_op jit(solution)/shard_map/all_to_all | solution.py:82
  12.5 0.6 dynamic-slice
  13.7 0.2 dynamic-update-slice
  13.9 12.4 %all-reduce = s32[64]{0:T(128)S(1)} all-reduce(s32[64]{0:T(128)S(1)} %dynamic-update-slice), channel_id=1, replica_groups=mesh['harm'=16,'bus'=2] {'harm'}, use_global_device_ids=true, to_apply=%add | all-reduce | flops 64 | bytes 512
  26.5 0.1 copy.61
  27.1 3.5 %scatter_fusion = f32[2,4,256,128]{3,1,2,0:T(4,128)S(1)} fusion(f32[2,4,256,128]{3,1,2,0:T(4,128)S(1)} %broadcast_in_dim.45, s32[64]{0:T(128)S(1)} %get-tuple-element.12, f32[64,2,4,128]{3,2,1,0:T(4,128)S(1)} %bitcast.149), kind=kCustom, calls=%fused_computation.13 | custom fusion | flops 65536 | bytes 786688 | tf_op jit(solution)/shard_map/scatter-add | solution.py:87
  30.6 0.2 convert_element_type.109
  30.8 0.7 fusion.31
  31.5 3.4 %collective-permute-start = (bf16[2,4,8,128]{3,1,2,0:T(4,128)(2,1)S(1)}, bf16[2,4,8,128]{3,1,2,0:T(4,128)(2,1)S(1)}, u32[]{:S(2)}, u32[]{:S(2)}) collective-permute-start(bf16[2,4,8,128]{3,1,2,0:T(4,128)(2,1)S(1)} %get-tuple-element.27), channel_id=1, source_target_pairs={{0,1},{2,3},{4,5},{6,7},{8,9},{10,11},{12,13},{14,15},{16,17},{18,... | collective-permute-start | bytes 49160 | tf_op jit(solution)/shard_map/ppermute | solution.py:25
  35.0 1.3 %collective-permute-start.1 = (bf16[2,4,8,128]{3,1,2,0:T(4,128)(2,1)S(1)}, bf16[2,4,8,128]{3,1,2,0:T(4,128)(2,1)S(1)}, u32[]{:S(2)}, u32[]{:S(2)}) collective-permute-start(bf16[2,4,8,128]{3,1,2,0:T(4,128)(2,1)S(1)} %get-tuple-element.28), channel_id=1, source_target_pairs={{1,0},{3,2},{5,4},{7,6},{9,8},{11,10},{13,12},{15,14},{17,16},{19,... | collective-permute-start | bytes 49160 | tf_op jit(solution)/shard_map/ppermute | solution.py:27
  36.4 0.1 copy.62
  36.6 0.1 copy.63
  36.7 0.1 copy.64
  37.2 3.4 %collective-permute-done.1 = bf16[2,4,8,128]{3,1,2,0:T(4,128)(2,1)S(1)} collective-permute-done((bf16[2,4,8,128]{3,1,2,0:T(4,128)(2,1)S(1)}, bf16[2,4,8,128]{3,1,2,0:T(4,128)(2,1)S(1)}, u32[]{:S(2)}, u32[]{:S(2)}) %collective-permute-start.1) | collective-permute-done | bytes 16416 | tf_op jit(solution)/shard_map/ppermute | solution.py:27
  40.6 0.5 pad_maximum_fusion
  41.1 0.2 slice_bitcast_fusion.2
  41.3 1.0 %gather_fusion.1 = bf16[256,4,128]{2,1,0:T(4,128)(2,1)S(1)} fusion(bf16[4,272,128]{2,0,1:T(4,128)(2,1)S(1)} %get-tuple-element.24, s32[1024]{0:T(1024)S(1)} %pad_clamp_fusion.3), kind=kCustom, calls=%fused_computation.clone | custom fusion | bytes 525312 | tf_op jit(solution)/shard_map/jit(_take)/gather | solution.py:51
  42.3 1.0 %gather_fusion.2 = bf16[256,4,128]{2,1,0:T(4,128)(2,1)S(1)} fusion(bf16[4,272,128]{2,0,1:T(4,128)(2,1)S(1)} %get-tuple-element.23, s32[1024]{0:T(1024)S(1)} %pad_clamp_fusion.3), kind=kCustom, calls=%fused_computation.1.clone | custom fusion | bytes 525312 | tf_op jit(solution)/shard_map/jit(_take)/gather | solution.py:52
  43.3 1.0 %gather_fusion.3 = bf16[256,4,128]{2,1,0:T(4,128)(2,1)S(1)} fusion(bf16[4,272,128]{2,0,1:T(4,128)(2,1)S(1)} %get-tuple-element.24, s32[1024]{0:T(1024)S(1)} %pad_clamp_fusion.2), kind=kCustom, calls=%fused_computation.2.clone | custom fusion | bytes 525312 | tf_op jit(solution)/shard_map/jit(_take)/gather | solution.py:51
  44.3 1.0 %gather_fusion.4 = bf16[256,4,128]{2,1,0:T(4,128)(2,1)S(1)} fusion(bf16[4,272,128]{2,0,1:T(4,128)(2,1)S(1)} %get-tuple-element.23, s32[1024]{0:T(1024)S(1)} %pad_clamp_fusion.2), kind=kCustom, calls=%fused_computation.3.clone | custom fusion | bytes 525312 | tf_op jit(solution)/shard_map/jit(_take)/gather | solution.py:52
  45.2 1.7 %gather_fusion.5 = bf16[256,4,128]{2,1,0:T(4,128)(2,1)} fusion(bf16[4,272,128]{2,0,1:T(4,128)(2,1)S(1)} %get-tuple-element.24, s32[1024]{0:T(1024)S(1)} %pad_clamp_fusion.1), kind=kCustom, calls=%fused_computation.4.clone | custom fusion | bytes 525312 | tf_op jit(solution)/shard_map/jit(_take)/gather | solution.py:51
  46.9 1.7 %gather_fusion.6 = bf16[256,4,128]{2,1,0:T(4,128)(2,1)} fusion(bf16[4,272,128]{2,0,1:T(4,128)(2,1)S(1)} %get-tuple-element.23, s32[1024]{0:T(1024)S(1)} %pad_clamp_fusion.1), kind=kCustom, calls=%fused_computation.5.clone | custom fusion | bytes 525312 | tf_op jit(solution)/shard_map/jit(_take)/gather | solution.py:52
  48.6 5.4 %fusion.37 = (bf16[1,4,256,128]{3,1,2,0:T(4,128)(2,1)S(1)}, f32[4,256,128]{2,0,1:T(4,128)S(1)}, f32[4,256,128]{2,0,1:T(4,128)S(1)}) fusion(f32[4,256]{0,1:T(8,128)S(1)} %copy.61, f32[4,256]{0,1:T(8,128)S(1)} %copy.53, bf16[256,4,128]{2,1,0:T(4,128)(2,1)} %gather_fusion.5, f32[4,256]{0,1:T(8,128)S(1)} %copy.66, bf16[256,4,128]{2,1,0:T(4,128)(2,1)} %gather_fusion.6, ...), kind=kLoop, calls=%fused_computation.96 | loop fusion | flops 5505024 | bytes 3441408 | tf_op jit(solution)/shard_map/stack | solution.py:97
  54.0 0.6 fusion.38
  54.6 1.6 %collective-permute-start.2 = (bf16[2,4,8,128]{3,1,2,0:T(4,128)(2,1)S(1)}, bf16[2,4,8,128]{3,1,2,0:T(4,128)(2,1)S(1)}, u32[]{:S(2)}, u32[]{:S(2)}) collective-permute-start(bf16[2,4,8,128]{3,1,2,0:T(4,128)(2,1)S(1)} %get-tuple-element.25), channel_id=1, source_target_pairs={{0,1},{2,3},{4,5},{6,7},{8,9},{10,11},{12,13},{14,15},{16,17},{18,... | collective-permute-start | bytes 49160 | tf_op jit(solution)/shard_map/ppermute | solution.py:25
  56.3 1.5 %collective-permute-start.3 = (bf16[2,4,8,128]{3,1,2,0:T(4,128)(2,1)S(1)}, bf16[2,4,8,128]{3,1,2,0:T(4,128)(2,1)S(1)}, u32[]{:S(2)}, u32[]{:S(2)}) collective-permute-start(bf16[2,4,8,128]{3,1,2,0:T(4,128)(2,1)S(1)} %get-tuple-element.26), channel_id=1, source_target_pairs={{1,0},{3,2},{5,4},{7,6},{9,8},{11,10},{13,12},{15,14},{17,16},{19,... | collective-permute-start | bytes 49160 | tf_op jit(solution)/shard_map/ppermute | solution.py:27
  57.8 4.1 %collective-permute-done.3 = bf16[2,4,8,128]{3,1,2,0:T(4,128)(2,1)S(1)} collective-permute-done((bf16[2,4,8,128]{3,1,2,0:T(4,128)(2,1)S(1)}, bf16[2,4,8,128]{3,1,2,0:T(4,128)(2,1)S(1)}, u32[]{:S(2)}, u32[]{:S(2)}) %collective-permute-start.3) | collective-permute-done | bytes 16416 | tf_op jit(solution)/shard_map/ppermute | solution.py:27
  61.9 0.5 pad_maximum_fusion.1
  62.4 0.2 slice_bitcast_fusion
  62.6 1.0 %gather_fusion.7 = bf16[256,4,128]{2,1,0:T(4,128)(2,1)S(1)} fusion(bf16[4,272,128]{2,0,1:T(4,128)(2,1)S(1)} %get-tuple-element.22, s32[1024]{0:T(1024)S(1)} %pad_clamp_fusion.3), kind=kCustom, calls=%fused_computation.6.clone | custom fusion | bytes 525312 | tf_op jit(solution)/shard_map/jit(_take)/gather | solution.py:51
  63.6 1.0 %gather_fusion.9 = bf16[256,4,128]{2,1,0:T(4,128)(2,1)S(1)} fusion(bf16[4,272,128]{2,0,1:T(4,128)(2,1)S(1)} %get-tuple-element.22, s32[1024]{0:T(1024)S(1)} %pad_clamp_fusion.2), kind=kCustom, calls=%fused_computation.8.clone | custom fusion | bytes 525312 | tf_op jit(solution)/shard_map/jit(_take)/gather | solution.py:51
  64.6 1.0 %gather_fusion.8 = bf16[256,4,128]{2,1,0:T(4,128)(2,1)S(1)} fusion(bf16[4,272,128]{2,0,1:T(4,128)(2,1)S(1)} %get-tuple-element.21, s32[1024]{0:T(1024)S(1)} %pad_clamp_fusion.3), kind=kCustom, calls=%fused_computation.7.clone | custom fusion | bytes 525312 | tf_op jit(solution)/shard_map/jit(_take)/gather | solution.py:52
  65.5 1.0 %gather_fusion.10 = bf16[256,4,128]{2,1,0:T(4,128)(2,1)S(1)} fusion(bf16[4,272,128]{2,0,1:T(4,128)(2,1)S(1)} %get-tuple-element.21, s32[1024]{0:T(1024)S(1)} %pad_clamp_fusion.2), kind=kCustom, calls=%fused_computation.9.clone | custom fusion | bytes 525312 | tf_op jit(solution)/shard_map/jit(_take)/gather | solution.py:52
  66.5 1.7 %gather_fusion.12 = bf16[256,4,128]{2,1,0:T(4,128)(2,1)} fusion(bf16[4,272,128]{2,0,1:T(4,128)(2,1)S(1)} %get-tuple-element.21, s32[1024]{0:T(1024)S(1)} %pad_clamp_fusion.1), kind=kCustom, calls=%fused_computation.11.clone | custom fusion | bytes 525312 | tf_op jit(solution)/shard_map/jit(_take)/gather | solution.py:52
  68.2 1.7 %gather_fusion.11 = bf16[256,4,128]{2,1,0:T(4,128)(2,1)} fusion(bf16[4,272,128]{2,0,1:T(4,128)(2,1)S(1)} %get-tuple-element.22, s32[1024]{0:T(1024)S(1)} %pad_clamp_fusion.1), kind=kCustom, calls=%fused_computation.10.clone | custom fusion | bytes 525312 | tf_op jit(solution)/shard_map/jit(_take)/gather | solution.py:51
  69.8 5.4 %fusion.39 = (bf16[1,4,256,128]{3,1,2,0:T(4,128)(2,1)S(1)}, f32[4,256,128]{2,0,1:T(4,128)S(1)}, f32[4,256,128]{2,0,1:T(4,128)S(1)}) fusion(f32[4,256]{0,1:T(8,128)S(1)} %copy.61, f32[4,256]{0,1:T(8,128)S(1)} %copy.53, bf16[256,4,128]{2,1,0:T(4,128)(2,1)} %gather_fusion.11, f32[4,256]{0,1:T(8,128)S(1)} %copy.66, bf16[256,4,128]{2,1,0:T(4,128)(2,1)} %gather_fusion.12, ...), kind=kLoop, calls=%fused_computation.98 | loop fusion | flops 5505024 | bytes 3441408 | tf_op jit(solution)/shard_map/stack | solution.py:108
  75.2 0.6 fusion.40
  75.9 0.4 pad_maximum_fusion.2
  76.2 0.7 gather_fusion
  77.0 0.8 select_bitcast_fusion
  77.8 3.5 %all-to-all-start.1 = ((bf16[2,4,64,128]{3,1,0,2:T(4,128)(2,1)}), bf16[2,4,64,128]{3,1,0,2:T(4,128)(2,1)S(1)}, u32[]{:S(2)}, u32[]{:S(2)}) async-start(bf16[2,4,64,128]{3,1,0,2:T(4,128)(2,1)} %select_bitcast_fusion), calls=%async_computation.1 | async-start | bytes 262144 | tf_op jit(solution)/shard_map/all_to_all | solution.py:110
  81.3 0.9 copy.69
  82.2 7.0 %all-to-all-done.1 = bf16[2,4,64,128]{3,1,0,2:T(4,128)(2,1)S(1)} async-done(((bf16[2,4,64,128]{3,1,0,2:T(4,128)(2,1)}), bf16[2,4,64,128]{3,1,0,2:T(4,128)(2,1)S(1)}, u32[]{:S(2)}, u32[]{:S(2)}) %all-to-all-start.1) | async-done | bytes 131104 | tf_op jit(solution)/shard_map/all_to_all | solution.py:110
  89.2 0.7 copy.68
  (38 shorter events, 1.1 us)
Async XLA Ops:
  0.6 2.1 %copy-start = (bf16[2,64,4,128]{3,2,1,0:T(4,128)(2,1)S(1)}, bf16[2,64,4,128]{3,2,1,0:T(4,128)(2,1)}, u32[]{:S(2)}) copy-start(bf16[2,64,4,128]{3,2,1,0:T(4,128)(2,1)} %param.9) | copy-start | bytes 393220
  2.8 9.6 %copy-start.2 = (s32[3,256]{1,0:T(4,128)S(1)}, s32[3,256]{1,0:T(4,128)}, u32[]{:S(2)}) copy-start(s32[3,256]{1,0:T(4,128)} %param.15) | copy-start | bytes 9220
  2.8 9.6 %copy-start.1 = (f32[2,4,4,256]{3,2,1,0:T(4,128)S(1)}, f32[2,4,4,256]{3,2,1,0:T(4,128)}, u32[]{:S(2)}) copy-start(f32[2,4,4,256]{3,2,1,0:T(4,128)} %param.14) | copy-start | bytes 98308
  2.8 9.7 %copy-start.4 = (u32[32]{0:T(128)S(1)}, u32[32]{0:T(128)}, u32[]{:S(2)}) copy-start(u32[32]{0:T(128)} %constant.65) | copy-start | bytes 388
  2.8 10.9 %copy-start.3 = (s32[4]{0:T(128)S(1)}, s32[4]{0:T(128)}, u32[]{:S(2)}) copy-start(s32[4]{0:T(128)} %param.13) | copy-start | bytes 52
  4.9 21.8 %all-to-all-start = ((bf16[2,64,4,128]{3,0,2,1:T(2,128)(2,1)}), bf16[2,64,4,128]{3,0,2,1:T(2,128)(2,1)S(1)}, u32[]{:S(2)}, u32[]{:S(2)}) async-start(bf16[2,64,4,128]{3,0,2,1:T(2,128)(2,1)} %copy.57), calls=%async_computation | async-start | bytes 262144 | tf_op jit(solution)/shard_map/all_to_all | solution.py:82
  31.5 5.6 %collective-permute-start = (bf16[2,4,8,128]{3,1,2,0:T(4,128)(2,1)S(1)}, bf16[2,4,8,128]{3,1,2,0:T(4,128)(2,1)S(1)}, u32[]{:S(2)}, u32[]{:S(2)}) collective-permute-start(bf16[2,4,8,128]{3,1,2,0:T(4,128)(2,1)S(1)} %get-tuple-element.27), channel_id=1, source_target_pairs={{0,1},{2,3},{4,5},{6,7},{8,9},{10,11},{12,13},{14,15},{16,17},{18,... | collective-permute-start | bytes 49160 | tf_op jit(solution)/shard_map/ppermute | solution.py:25
  35.0 5.6 %collective-permute-start.1 = (bf16[2,4,8,128]{3,1,2,0:T(4,128)(2,1)S(1)}, bf16[2,4,8,128]{3,1,2,0:T(4,128)(2,1)S(1)}, u32[]{:S(2)}, u32[]{:S(2)}) collective-permute-start(bf16[2,4,8,128]{3,1,2,0:T(4,128)(2,1)S(1)} %get-tuple-element.28), channel_id=1, source_target_pairs={{1,0},{3,2},{5,4},{7,6},{9,8},{11,10},{13,12},{15,14},{17,16},{19,... | collective-permute-start | bytes 49160 | tf_op jit(solution)/shard_map/ppermute | solution.py:27
  54.6 3.1 %collective-permute-start.2 = (bf16[2,4,8,128]{3,1,2,0:T(4,128)(2,1)S(1)}, bf16[2,4,8,128]{3,1,2,0:T(4,128)(2,1)S(1)}, u32[]{:S(2)}, u32[]{:S(2)}) collective-permute-start(bf16[2,4,8,128]{3,1,2,0:T(4,128)(2,1)S(1)} %get-tuple-element.25), channel_id=1, source_target_pairs={{0,1},{2,3},{4,5},{6,7},{8,9},{10,11},{12,13},{14,15},{16,17},{18,... | collective-permute-start | bytes 49160 | tf_op jit(solution)/shard_map/ppermute | solution.py:25
  56.3 5.6 %collective-permute-start.3 = (bf16[2,4,8,128]{3,1,2,0:T(4,128)(2,1)S(1)}, bf16[2,4,8,128]{3,1,2,0:T(4,128)(2,1)S(1)}, u32[]{:S(2)}, u32[]{:S(2)}) collective-permute-start(bf16[2,4,8,128]{3,1,2,0:T(4,128)(2,1)S(1)} %get-tuple-element.26), channel_id=1, source_target_pairs={{1,0},{3,2},{5,4},{7,6},{9,8},{11,10},{13,12},{15,14},{17,16},{19,... | collective-permute-start | bytes 49160 | tf_op jit(solution)/shard_map/ppermute | solution.py:27
  77.8 11.4 %all-to-all-start.1 = ((bf16[2,4,64,128]{3,1,0,2:T(4,128)(2,1)}), bf16[2,4,64,128]{3,1,0,2:T(4,128)(2,1)S(1)}, u32[]{:S(2)}, u32[]{:S(2)}) async-start(bf16[2,4,64,128]{3,1,0,2:T(4,128)(2,1)} %select_bitcast_fusion), calls=%async_computation.1 | async-start | bytes 262144 | tf_op jit(solution)/shard_map/all_to_all | solution.py:110
where the time goes:
time: 91.1 us; the launch traced here: 89.9 us
  other arithmetic  20.9 us (23%)
  local copies, waits for them, and re-layouts  20.1 us (22%)
  starting transfers between devices  18.7 us (21%)
  waiting for transfers between devices  14.6 us (16%)
  blocking collectives  12.4 us (14%)
  between operations  1.79 us (2%)
  matrix products  1.34 us (1%)
    unnamed x1, blocking collectives  12.4 us
    ppermute x2, waiting for transfers between devices, extended_2(): lax.ppermute(head, axis, [((i + 1) % count, i) for i in range(ends)])  7.56 us
    all_to_all x1, starting transfers between devices, local(): lax.all_to_all(spectra, 'harm', split_axis=1, concat_axis=2, tiled=True)  7.38 us
    gather x6, local copies, waits for them, and re-layouts, line_sum(): near_real = jnp.take(volt_real, targets[line_num], axis=1)  7.25 us
    gather x6, local copies, waits for them, and re-layouts, line_sum(): near_imag = jnp.take(volt_imag, targets[line_num], axis=1)  7.24 us
    all_to_all x1, waiting for transfers between devices, local(): lax.all_to_all(picked, 'harm', split_axis=2, concat_axis=1, tiled=True)  7.01 us
    another operation x3, other arithmetic, local(): bus_volt = jnp.stack([volt_real, volt_imag]).astype(jnp.bfloat16)  6.37 us
    another operation x2, other arithmetic, local(): jnp.stack([volt_real, volt_imag])  6 us
  transfers between devices with their start and end apart: 6, of which 3 were waited for; matrix products, arithmetic and copies ran while one was open for 3% of the time, Pallas kernels for 0%

commit v1 on v0

--- a/solution.py
+++ b/solution.py
@@ -79,7 +79,9 @@
     ) * NT ** (-0.5)
     pieces = spectra.astype(jnp.bfloat16)
     spectra = pieces.reshape(2, H, conv_count, snapshots)
-    received = lax.all_to_all(spectra, "harm", split_axis=1, concat_axis=2, tiled=True)
+    cells_2 = jnp.split(spectra, lax.axis_size("harm"), axis=1)
+    incoming = lax.all_to_all(jnp.stack(cells_2), "harm", 0, 0)
+    received = jnp.concatenate(incoming, axis=2)
     block_bus = lax.all_gather(conv_bus, "harm", axis=0, tiled=True) - first_bus
     summed = (
         jnp.zeros((2, received.shape[1], block_rows, snapshots), jnp.float32)

time: 91.1 us -> 98.1 us (1.077)
  local copies, waits for them, and re-layouts: 20.1 us -> 27.2 us
    unnamed x14 -> x39, local copies, waits for them, and re-layouts: 1.73 us -> 10.8 us
    gather x6, local copies, waits for them, and re-layouts: 7.25 us -> 6.02 us  [line_sum(): near_real = jnp.take(volt_real, targets[line_num], axis=1)]
  transfers between devices with their start and end apart: 6 -> 6, of which waited for: 3 -> 3; matrix products, arithmetic and copies ran while one was open for 3% -> 4% of each run, Pallas kernels for 0% -> 0%
where the time goes in v1:
time: 98.1 us; the launch traced here: 97.2 us
  local copies, waits for them, and re-layouts  27.2 us (28%)
  other arithmetic  21 us (21%)
  starting transfers between devices  18.7 us (19%)
  waiting for transfers between devices  14.6 us (15%)
  blocking collectives  12.4 us (13%)
  between operations  1.85 us (2%)
  matrix products  1.47 us (1%)
    unnamed x1, blocking collectives  12.4 us
    unnamed x39, local copies, waits for them, and re-layouts  10.8 us
    ppermute x2, waiting for transfers between devices, extended_2(): lax.ppermute(head, axis, [((i + 1) % count, i) for i in range(ends)])  7.56 us
    all_to_all x1, starting transfers between devices, local(): incoming = lax.all_to_all(jnp.stack(cells_2), 'harm', 0, 0)  7.38 us
    all_to_all x1, waiting for transfers between devices, local(): lax.all_to_all(picked, 'harm', split_axis=2, concat_axis=1, tiled=True)  7.01 us
    gather x6, local copies, waits for them, and re-layouts, line_sum(): near_imag = jnp.take(volt_imag, targets[line_num], axis=1)  6.57 us
    gather x6, local copies, waits for them, and re-layouts, line_sum(): near_real = jnp.take(volt_real, targets[line_num], axis=1)  6.02 us
    another operation x2, other arithmetic, local(): jnp.stack([volt_real, volt_imag])  5.95 us
  transfers between devices with their start and end apart: 6, of which 3 were waited for; matrix products, arithmetic and copies ran while one was open for 4% of the time, Pallas kernels for 0%

profile of v1, /device:TPU:0, one launch (start us, length us, event | category | flops | bytes accessed | tf_op | source)
XLA Modules:
  0.0 97.2 jit_solution(3293214078848983362)
XLA Ops:
  0.7 1.2 %cosine_convert_fusion = (bf16[64,1024]{1,0:T(8,128)(2,1)S(1)}, bf16[64,1024]{1,0:T(8,128)(2,1)S(1)}) fusion(s32[64]{0:T(128)S(1)} %iota_add_fusion.1), kind=kLoop, calls=%fused_computation.104 | loop fusion | flops 1114112 | bytes 262400 | tf_op jit(solution)/shard_map/convert.14
  1.9 0.9 select_reduce_fusion
  2.8 1.5 %fusion.3 = bf16[128,4,128]{2,0,1:T(8,128)(2,1)S(1)} fusion(f32[4]{0:T(128)S(1)} %select_reduce_fusion, f32[4,128]{1,0:T(4,128)} %param.10, bf16[64,1024]{1,0:T(8,128)(2,1)S(1)} %get-tuple-element.37, bf16[64,1024]{1,0:T(8,128)(2,1)S(1)} %get-tuple-element.36, bf16[128,4,128]{2,1,0:T(4,128)(2,1)S(1)} %bitcast.209), kind=kOutput, calls=%fused_computation.18 | convolution fusion | flops 271187968 | bytes 526352 | tf_op jit(solution)/shard_map/csn,kn->kcs/dot_general | solution.py:77
  4.3 0.6 constant_dynamic-update-slice_fusion.15
  4.9 0.6 constant_dynamic-update-slice_fusion.14
  5.5 0.6 constant_dynamic-update-slice_fusion.13
  6.1 0.6 constant_dynamic-update-slice_fusion.12
  6.7 0.6 constant_dynamic-update-slice_fusion.11
  7.3 0.6 constant_dynamic-update-slice_fusion.10
  7.9 0.6 constant_dynamic-update-slice_fusion.9
  8.5 0.6 constant_dynamic-update-slice_fusion.8
  9.7 0.6 constant_dynamic-update-slice_fusion.6
  10.3 0.6 constant_dynamic-update-slice_fusion.5
  11.0 0.6 constant_dynamic-update-slice_fusion.4
  12.2 0.6 constant_dynamic-update-slice_fusion.2
  13.4 0.6 constant_dynamic-update-slice_fusion
  14.0 7.4 %all-to-all-start = ((bf16[16,2,4,4,128]{4,2,1,3,0:T(4,128)(2,1)}), bf16[16,2,4,4,128]{4,2,1,3,0:T(4,128)(2,1)S(1)}, u32[]{:S(2)}, u32[]{:S(2)}) async-start(bf16[16,2,4,4,128]{4,2,1,3,0:T(4,128)(2,1)} %constant_dynamic-update-slice_fusion), calls=%async_computation | async-start | bytes 262144 | tf_op jit(solution)/shard_map/all_to_all | solution.py:83
  23.0 12.4 %all-reduce = s32[64]{0:T(128)S(1)} all-reduce(s32[64]{0:T(128)S(1)} %dynamic-update-slice), channel_id=1, replica_groups=mesh['harm'=16,'bus'=2] {'harm'}, use_global_device_ids=true, to_apply=%add | all-reduce | flops 64 | bytes 512
  37.0 3.5 %scatter_fusion = f32[2,4,256,128]{3,1,2,0:T(4,128)S(1)} fusion(f32[2,4,256,128]{3,1,2,0:T(4,128)S(1)} %broadcast_in_dim.45, s32[64]{0:T(128)S(1)} %get-tuple-element.8, f32[64,2,4,128]{3,2,1,0:T(4,128)S(1)} %bitcast.210), kind=kCustom, calls=%fused_computation.13 | custom fusion | flops 65536 | bytes 786688 | tf_op jit(solution)/shard_map/scatter-add | solution.py:89
  40.7 0.7 fusion.31
  41.5 3.4 %collective-permute-start = (bf16[2,4,8,128]{3,1,2,0:T(4,128)(2,1)S(1)}, bf16[2,4,8,128]{3,1,2,0:T(4,128)(2,1)S(1)}, u32[]{:S(2)}, u32[]{:S(2)}) collective-permute-start(bf16[2,4,8,128]{3,1,2,0:T(4,128)(2,1)S(1)} %get-tuple-element.23), channel_id=1, source_target_pairs={{0,1},{2,3},{4,5},{6,7},{8,9},{10,11},{12,13},{14,15},{16,17},{18,... | collective-permute-start | bytes 49160 | tf_op jit(solution)/shard_map/ppermute | solution.py:25
  44.9 1.3 %collective-permute-start.1 = (bf16[2,4,8,128]{3,1,2,0:T(4,128)(2,1)S(1)}, bf16[2,4,8,128]{3,1,2,0:T(4,128)(2,1)S(1)}, u32[]{:S(2)}, u32[]{:S(2)}) collective-permute-start(bf16[2,4,8,128]{3,1,2,0:T(4,128)(2,1)S(1)} %get-tuple-element.24), channel_id=1, source_target_pairs={{1,0},{3,2},{5,4},{7,6},{9,8},{11,10},{13,12},{15,14},{17,16},{19,... | collective-permute-start | bytes 49160 | tf_op jit(solution)/shard_map/ppermute | solution.py:27
  47.2 3.4 %collective-permute-done.1 = bf16[2,4,8,128]{3,1,2,0:T(4,128)(2,1)S(1)} collective-permute-done((bf16[2,4,8,128]{3,1,2,0:T(4,128)(2,1)S(1)}, bf16[2,4,8,128]{3,1,2,0:T(4,128)(2,1)S(1)}, u32[]{:S(2)}, u32[]{:S(2)}) %collective-permute-start.1) | collective-permute-done | bytes 16416 | tf_op jit(solution)/shard_map/ppermute | solution.py:27
  51.3 1.0 %gather_fusion.6 = bf16[256,4,128]{2,1,0:T(4,128)(2,1)S(1)} fusion(bf16[4,272,128]{2,0,1:T(4,128)(2,1)S(1)} %get-tuple-element.19, s32[1024]{0:T(1024)S(1)} %get-tuple-element.39), kind=kCustom, calls=%fused_computation.5.clone | custom fusion | bytes 525312 | tf_op jit(solution)/shard_map/jit(_take)/gather | solution.py:52
  52.2 1.0 %gather_fusion.4 = bf16[256,4,128]{2,1,0:T(4,128)(2,1)S(1)} fusion(bf16[4,272,128]{2,0,1:T(4,128)(2,1)S(1)} %get-tuple-element.19, s32[1024]{0:T(1024)S(1)} %get-tuple-element.40), kind=kCustom, calls=%fused_computation.3.clone | custom fusion | bytes 525312 | tf_op jit(solution)/shard_map/jit(_take)/gather | solution.py:52
  53.2 1.0 %gather_fusion.5 = bf16[256,4,128]{2,1,0:T(4,128)(2,1)S(1)} fusion(bf16[4,272,128]{2,0,1:T(4,128)(2,1)S(1)} %get-tuple-element.20, s32[1024]{0:T(1024)S(1)} %get-tuple-element.39), kind=kCustom, calls=%fused_computation.4.clone | custom fusion | bytes 525312 | tf_op jit(solution)/shard_map/jit(_take)/gather | solution.py:51
  54.2 1.0 %gather_fusion.3 = bf16[256,4,128]{2,1,0:T(4,128)(2,1)S(1)} fusion(bf16[4,272,128]{2,0,1:T(4,128)(2,1)S(1)} %get-tuple-element.20, s32[1024]{0:T(1024)S(1)} %get-tuple-element.40), kind=kCustom, calls=%fused_computation.2.clone | custom fusion | bytes 525312 | tf_op jit(solution)/shard_map/jit(_take)/gather | solution.py:51
  55.2 1.7 %gather_fusion.2 = bf16[256,4,128]{2,1,0:T(4,128)(2,1)} fusion(bf16[4,272,128]{2,0,1:T(4,128)(2,1)S(1)} %get-tuple-element.19, s32[1024]{0:T(1024)S(1)} %get-tuple-element.41), kind=kCustom, calls=%fused_computation.1.clone | custom fusion | bytes 525312 | tf_op jit(solution)/shard_map/jit(_take)/gather | solution.py:52
  56.9 1.0 %gather_fusion.1 = bf16[256,4,128]{2,1,0:T(4,128)(2,1)S(1)} fusion(bf16[4,272,128]{2,0,1:T(4,128)(2,1)S(1)} %get-tuple-element.20, s32[1024]{0:T(1024)S(1)} %get-tuple-element.41), kind=kCustom, calls=%fused_computation.clone | custom fusion | bytes 525312 | tf_op jit(solution)/shard_map/jit(_take)/gather | solution.py:51
  57.9 5.3 %fusion.37 = (bf16[1,4,256,128]{3,1,2,0:T(4,128)(2,1)S(1)}, f32[4,256,128]{2,0,1:T(4,128)S(1)}, f32[4,256,128]{2,0,1:T(4,128)S(1)}) fusion(f32[4,256]{0,1:T(8,128)S(1)} %copy.24, f32[4,256]{0,1:T(8,128)S(1)} %copy.21, bf16[256,4,128]{2,1,0:T(4,128)(2,1)S(1)} %gather_fusion.5, f32[4,256]{0,1:T(8,128)S(1)} %copy.29, bf16[256,4,128]{2,1,0:T(4,128)(2,1)S(1)} %gather_fusion.6, ...), kind=kLoop, calls=%fused_computation.96 | loop fusion | flops 5505024 | bytes 3441408 | tf_op jit(solution)/shard_map/stack | solution.py:99
  63.2 0.6 fusion.38
  63.9 1.6 %collective-permute-start.2 = (bf16[2,4,8,128]{3,1,2,0:T(4,128)(2,1)S(1)}, bf16[2,4,8,128]{3,1,2,0:T(4,128)(2,1)S(1)}, u32[]{:S(2)}, u32[]{:S(2)}) collective-permute-start(bf16[2,4,8,128]{3,1,2,0:T(4,128)(2,1)S(1)} %get-tuple-element.21), channel_id=1, source_target_pairs={{0,1},{2,3},{4,5},{6,7},{8,9},{10,11},{12,13},{14,15},{16,17},{18,... | collective-permute-start | bytes 49160 | tf_op jit(solution)/shard_map/ppermute | solution.py:25
  65.5 1.5 %collective-permute-start.3 = (bf16[2,4,8,128]{3,1,2,0:T(4,128)(2,1)S(1)}, bf16[2,4,8,128]{3,1,2,0:T(4,128)(2,1)S(1)}, u32[]{:S(2)}, u32[]{:S(2)}) collective-permute-start(bf16[2,4,8,128]{3,1,2,0:T(4,128)(2,1)S(1)} %get-tuple-element.22), channel_id=1, source_target_pairs={{1,0},{3,2},{5,4},{7,6},{9,8},{11,10},{13,12},{15,14},{17,16},{19,... | collective-permute-start | bytes 49160 | tf_op jit(solution)/shard_map/ppermute | solution.py:27
  67.0 4.1 %collective-permute-done.3 = bf16[2,4,8,128]{3,1,2,0:T(4,128)(2,1)S(1)} collective-permute-done((bf16[2,4,8,128]{3,1,2,0:T(4,128)(2,1)S(1)}, bf16[2,4,8,128]{3,1,2,0:T(4,128)(2,1)S(1)}, u32[]{:S(2)}, u32[]{:S(2)}) %collective-permute-start.3) | collective-permute-done | bytes 16416 | tf_op jit(solution)/shard_map/ppermute | solution.py:27
  71.8 1.0 %gather_fusion.12 = bf16[256,4,128]{2,1,0:T(4,128)(2,1)S(1)} fusion(bf16[4,272,128]{2,0,1:T(4,128)(2,1)S(1)} %get-tuple-element.17, s32[1024]{0:T(1024)S(1)} %get-tuple-element.39), kind=kCustom, calls=%fused_computation.11.clone | custom fusion | bytes 525312 | tf_op jit(solution)/shard_map/jit(_take)/gather | solution.py:52
  72.8 1.0 %gather_fusion.10 = bf16[256,4,128]{2,1,0:T(4,128)(2,1)S(1)} fusion(bf16[4,272,128]{2,0,1:T(4,128)(2,1)S(1)} %get-tuple-element.17, s32[1024]{0:T(1024)S(1)} %get-tuple-element.40), kind=kCustom, calls=%fused_computation.9.clone | custom fusion | bytes 525312 | tf_op jit(solution)/shard_map/jit(_take)/gather | solution.py:52
  73.8 1.0 %gather_fusion.8 = bf16[256,4,128]{2,1,0:T(4,128)(2,1)S(1)} fusion(bf16[4,272,128]{2,0,1:T(4,128)(2,1)S(1)} %get-tuple-element.17, s32[1024]{0:T(1024)S(1)} %get-tuple-element.41), kind=kCustom, calls=%fused_computation.7.clone | custom fusion | bytes 525312 | tf_op jit(solution)/shard_map/jit(_take)/gather | solution.py:52
  74.8 1.0 %gather_fusion.11 = bf16[256,4,128]{2,1,0:T(4,128)(2,1)S(1)} fusion(bf16[4,272,128]{2,0,1:T(4,128)(2,1)S(1)} %get-tuple-element.18, s32[1024]{0:T(1024)S(1)} %get-tuple-element.39), kind=kCustom, calls=%fused_computation.10.clone | custom fusion | bytes 525312 | tf_op jit(solution)/shard_map/jit(_take)/gather | solution.py:51
  75.8 1.0 %gather_fusion.7 = bf16[256,4,128]{2,1,0:T(4,128)(2,1)S(1)} fusion(bf16[4,272,128]{2,0,1:T(4,128)(2,1)S(1)} %get-tuple-element.18, s32[1024]{0:T(1024)S(1)} %get-tuple-element.41), kind=kCustom, calls=%fused_computation.6.clone | custom fusion | bytes 525312 | tf_op jit(solution)/shard_map/jit(_take)/gather | solution.py:51
  76.8 1.1 %gather_fusion.9 = bf16[256,4,128]{2,1,0:T(4,128)(2,1)S(1)} fusion(bf16[4,272,128]{2,0,1:T(4,128)(2,1)S(1)} %get-tuple-element.18, s32[1024]{0:T(1024)} %copy-done.2), kind=kCustom, calls=%fused_computation.8.clone | custom fusion | bytes 525312 | tf_op jit(solution)/shard_map/jit(_take)/gather | solution.py:51
  77.9 4.5 %fusion.39 = (bf16[1,4,256,128]{3,1,2,0:T(4,128)(2,1)S(1)}, f32[4,256,128]{2,0,1:T(4,128)S(1)}, f32[4,256,128]{2,0,1:T(4,128)S(1)}) fusion(f32[4,256]{0,1:T(8,128)S(1)} %copy.24, f32[4,256]{0,1:T(8,128)S(1)} %copy.21, bf16[256,4,128]{2,1,0:T(4,128)(2,1)S(1)} %gather_fusion.11, f32[4,256]{0,1:T(8,128)S(1)} %copy.29, ...), kind=kLoop, calls=%fused_computation.98 | loop fusion | flops 5505024 | bytes 3441408 | tf_op jit(solution)/shard_map/stack | solution.py:110
  82.4 0.6 fusion.40
  83.4 0.8 gather_fusion
  84.3 0.8 select_bitcast_fusion
  85.1 3.5 %all-to-all-start.1 = ((bf16[2,4,64,128]{3,1,0,2:T(4,128)(2,1)}), bf16[2,4,64,128]{3,1,0,2:T(4,128)(2,1)S(1)}, u32[]{:S(2)}, u32[]{:S(2)}) async-start(bf16[2,4,64,128]{3,1,0,2:T(4,128)(2,1)} %select_bitcast_fusion), calls=%async_computation.1 | async-start | bytes 262144 | tf_op jit(solution)/shard_map/all_to_all | solution.py:112
  88.6 0.9 copy.32
  89.5 7.0 %all-to-all-done.1 = bf16[2,4,64,128]{3,1,0,2:T(4,128)(2,1)S(1)} async-done(((bf16[2,4,64,128]{3,1,0,2:T(4,128)(2,1)}), bf16[2,4,64,128]{3,1,0,2:T(4,128)(2,1)S(1)}, u32[]{:S(2)}, u32[]{:S(2)}) %all-to-all-start.1) | async-done | bytes 131104 | tf_op jit(solution)/shard_map/all_to_all | solution.py:112
  96.5 0.7 copy.31
  (60 shorter events, 7.1 us)
Async XLA Ops:
  0.6 2.1 %copy-start = (bf16[2,64,4,128]{3,2,1,0:T(4,128)(2,1)S(1)}, bf16[2,64,4,128]{3,2,1,0:T(4,128)(2,1)}, u32[]{:S(2)}) copy-start(bf16[2,64,4,128]{3,2,1,0:T(4,128)(2,1)} %param.9) | copy-start | bytes 393220
  2.8 18.6 %copy-start.5 = (s32[3,256]{1,0:T(4,128)S(1)}, s32[3,256]{1,0:T(4,128)}, u32[]{:S(2)}) copy-start(s32[3,256]{1,0:T(4,128)} %param.15) | copy-start | bytes 9220
  2.8 18.7 %copy-start.9 = (u32[32]{0:T(128)S(1)}, u32[32]{0:T(128)}, u32[]{:S(2)}) copy-start(u32[32]{0:T(128)} %constant.65) | copy-start | bytes 388
  2.8 19.9 %copy-start.8 = (s32[4]{0:T(128)S(1)}, s32[4]{0:T(128)}, u32[]{:S(2)}) copy-start(s32[4]{0:T(128)} %param.13) | copy-start | bytes 52
  2.8 32.6 %copy-start.1 = (f32[2,4,4,256]{3,2,1,0:T(4,128)S(1)}, f32[2,4,4,256]{3,2,1,0:T(4,128)}, u32[]{:S(2)}) copy-start(f32[2,4,4,256]{3,2,1,0:T(4,128)} %param.14) | copy-start | bytes 98308
  14.0 22.9 %all-to-all-start = ((bf16[16,2,4,4,128]{4,2,1,3,0:T(4,128)(2,1)}), bf16[16,2,4,4,128]{4,2,1,3,0:T(4,128)(2,1)S(1)}, u32[]{:S(2)}, u32[]{:S(2)}) async-start(bf16[16,2,4,4,128]{4,2,1,3,0:T(4,128)(2,1)} %constant_dynamic-update-slice_fusion), calls=%async_computation | async-start | bytes 262144 | tf_op jit(solution)/shard_map/all_to_all | solution.py:83
  21.4 36.4 %copy-start.7 = (pred[256]{0:T(512)(128)(4,1)}, pred[256]{0:T(512)(128)(4,1)S(1)}, u32[]{:S(2)}) copy-start(pred[256]{0:T(512)(128)(4,1)S(1)} %compare_and_fusion.2) | copy-start | bytes 772
  36.8 21.1 %copy-start.3 = (pred[256]{0:T(512)(128)(4,1)}, pred[256]{0:T(512)(128)(4,1)S(1)}, u32[]{:S(2)}) copy-start(pred[256]{0:T(512)(128)(4,1)S(1)} %get-tuple-element.42) | copy-start | bytes 772
  36.8 21.1 %copy-start.4 = (pred[256]{0:T(512)(128)(4,1)}, pred[256]{0:T(512)(128)(4,1)S(1)}, u32[]{:S(2)}) copy-start(pred[256]{0:T(512)(128)(4,1)S(1)} %get-tuple-element.43) | copy-start | bytes 772
  41.5 5.7 %collective-permute-start = (bf16[2,4,8,128]{3,1,2,0:T(4,128)(2,1)S(1)}, bf16[2,4,8,128]{3,1,2,0:T(4,128)(2,1)S(1)}, u32[]{:S(2)}, u32[]{:S(2)}) collective-permute-start(bf16[2,4,8,128]{3,1,2,0:T(4,128)(2,1)S(1)} %get-tuple-element.23), channel_id=1, source_target_pairs={{0,1},{2,3},{4,5},{6,7},{8,9},{10,11},{12,13},{14,15},{16,17},{18,... | collective-permute-start | bytes 49160 | tf_op jit(solution)/shard_map/ppermute | solution.py:25
  44.9 5.6 %collective-permute-start.1 = (bf16[2,4,8,128]{3,1,2,0:T(4,128)(2,1)S(1)}, bf16[2,4,8,128]{3,1,2,0:T(4,128)(2,1)S(1)}, u32[]{:S(2)}, u32[]{:S(2)}) collective-permute-start(bf16[2,4,8,128]{3,1,2,0:T(4,128)(2,1)S(1)} %get-tuple-element.24), channel_id=1, source_target_pairs={{1,0},{3,2},{5,4},{7,6},{9,8},{11,10},{13,12},{15,14},{17,16},{19,... | collective-permute-start | bytes 49160 | tf_op jit(solution)/shard_map/ppermute | solution.py:27
  46.3 26.6 %copy-start.2 = (s32[1024]{0:T(1024)}, s32[1024]{0:T(1024)S(1)}, u32[]{:S(2)}) copy-start(s32[1024]{0:T(1024)S(1)} %get-tuple-element.40) | copy-start | bytes 12292
  63.9 3.1 %collective-permute-start.2 = (bf16[2,4,8,128]{3,1,2,0:T(4,128)(2,1)S(1)}, bf16[2,4,8,128]{3,1,2,0:T(4,128)(2,1)S(1)}, u32[]{:S(2)}, u32[]{:S(2)}) collective-permute-start(bf16[2,4,8,128]{3,1,2,0:T(4,128)(2,1)S(1)} %get-tuple-element.21), channel_id=1, source_target_pairs={{0,1},{2,3},{4,5},{6,7},{8,9},{10,11},{12,13},{14,15},{16,17},{18,... | collective-permute-start | bytes 49160 | tf_op jit(solution)/shard_map/ppermute | solution.py:25
  65.5 5.6 %collective-permute-start.3 = (bf16[2,4,8,128]{3,1,2,0:T(4,128)(2,1)S(1)}, bf16[2,4,8,128]{3,1,2,0:T(4,128)(2,1)S(1)}, u32[]{:S(2)}, u32[]{:S(2)}) collective-permute-start(bf16[2,4,8,128]{3,1,2,0:T(4,128)(2,1)S(1)} %get-tuple-element.22), channel_id=1, source_target_pairs={{1,0},{3,2},{5,4},{7,6},{9,8},{11,10},{13,12},{15,14},{17,16},{19,... | collective-permute-start | bytes 49160 | tf_op jit(solution)/shard_map/ppermute | solution.py:27
  83.0 1.2 %copy-start.6 = (pred[64]{0:T(512)(128)(4,1)S(1)}, pred[64]{0:T(512)(128)(4,1)}, u32[]{:S(2)}) copy-start(pred[64]{0:T(512)(128)(4,1)} %get-tuple-element.7) | copy-start | bytes 196
  85.1 11.4 %all-to-all-start.1 = ((bf16[2,4,64,128]{3,1,0,2:T(4,128)(2,1)}), bf16[2,4,64,128]{3,1,0,2:T(4,128)(2,1)S(1)}, u32[]{:S(2)}, u32[]{:S(2)}) async-start(bf16[2,4,64,128]{3,1,0,2:T(4,128)(2,1)} %select_bitcast_fusion), calls=%async_computation.1 | async-start | bytes 262144 | tf_op jit(solution)/shard_map/all_to_all | solution.py:112
